TPU v7x, 32 devices: a whole 2x2x4 slice. The times are simulated.
32 devices in a mesh: psg: 8 (over z, x), mp: 4 (over y, core).
Axes of the slice: x: 2, y: 2, z: 4, core: 2. Of those that a mesh axis runs over, the one named last changes fastest.
Arguments:
- tokens: bfloat16 [8192, 4096], P('psg'), may hold values from -6 to 6
- lengths: int32 [32], P('psg'), may hold values from 32 to 256, as said below
- assignment: int32 [32], P('psg'), may hold values from 0 to 3, as said below
- retrieval: float32 [32], P('psg'), may hold values from -8 to 306
- enc_gain: float32 [4096], replicated, may hold values from 0.25 to 1.75
- enc_qkv: bfloat16 [3, 4096, 2048], P(None, 'psg', 'mp'), may hold values from -0.09375 to 0.09375
- position_bias: float32 [32, 32], P('mp'), may hold values from -6 to 306
- enc_output: bfloat16 [2048, 4096], P('mp', 'psg'), may hold values from -0.125 to 0.125
- final_gain: float32 [4096], replicated, may hold values from 0.25 to 1.75
- embedding: bfloat16 [32128, 4096], P('mp', 'psg'), may hold values from -18 to 18
- dec_tokens: int32 [4, 2], replicated, may hold values from 0 to 32127
- dec_gain: float32 [4096], P('psg'), may hold values from 0.25 to 1.75
- cross_query: bfloat16 [4096, 2048], P('psg', 'mp'), may hold values from -0.0234375 to 0.0234375
- cross_keyval: bfloat16 [2, 4096, 2048], P(None, 'psg', 'mp'), may hold values from -0.09375 to 0.09375
- cross_output: bfloat16 [2048, 4096], P('mp', 'psg'), may hold values from -0.25 to 0.25
Outputs:
- encoded: bfloat16 [8192, 4096], P('psg', 'mp')
- decoded: bfloat16 [4, 2, 4096], P(None, None, ('psg', 'mp'))
Inputs may be any that keep to these rules, and one draw needn't show every extreme that they name: Passage p holds real tokens in its first lengths[p] slots and padding after them; in every draw all passages of some index of psg have 256 real tokens. `assignment`: every claim has exactly 8 passages.
All inputs are finite; a program needn't handle non-finite values.
Results may differ from a plain program's by a relative error of at most 0.013.
The roundings to bfloat16 on the way count: a program that leaves them out, or rounds other values in their place, can miss the bound.
Values may be sent and summed in bfloat16 or wider, within the bound.
No kernel may reach another device: no remote copies, remote signals or barrier semaphores. Data moves between devices by JAX's collectives and lax.ppermute only.
A program may use at most 128 MiB of HBM per device.

v0:
```python
import math
import jax
import jax.numpy as jnp
import numpy as np
from jax import lax
from jax.sharding import PartitionSpec as P

D = 4096
HEAD_DIM = 64
BUCKETS = 32
MAXDIST = 128
SEQ = 256
CLAIMS = 4
POS = 2
EPSILON = 1e-06
MASKED = -1e30
HIGHEST = lax.Precision.HIGHEST


def merged(value, axis, combine):
    everything = jax.tree.map(lambda part: lax.all_gather(part, axis), value)
    first = jax.tree.map(lambda part: part[0], everything)

    def turn(k, so_far):
        return combine(so_far, jax.tree.map(lambda part: part[k], everything))

    return lax.fori_loop(1, lax.axis_size(axis), turn, first)


def bucket_onehot(length, buckets, max_distance):
    halfway = buckets // 2
    exact_max = halfway // 2
    relative_list = list(range(-(length - 1), length))
    beyond_list = [
        min(
            halfway - 1,
            exact_max
            + math.floor(
                math.log(max(abs(shift), 1) / exact_max)
                / math.log(max_distance / exact_max)
                * (halfway - exact_max)
            ),
        )
        for shift in relative_list
    ]
    relative = np.array(relative_list)
    beyond = np.array(beyond_list)
    distance = np.abs(relative)
    bucket_ids = np.where(relative > 0, halfway, 0) + np.where(
        distance < exact_max, distance, beyond
    )
    return (bucket_ids[None, :] == np.arange(buckets)[:, None]).astype(np.float32)


def toeplitz(vectors):
    heads_count, width_all = vectors.shape
    length = (width_all + 1) // 2
    padded = jnp.concatenate([vectors, jnp.zeros((heads_count, 1), vectors.dtype)], axis=1)
    rolled = jnp.roll(padded, -(length - 1), axis=1)
    repeated = jnp.tile(rolled, (1, length))[:, : length * (2 * length - 1)]
    return repeated.reshape(heads_count, length, 2 * length - 1)[:, :, :length]


def rms_norm(values, norm_gain):
    values = values.astype(jnp.float32)
    inverse = lax.rsqrt(jnp.mean(values * values, axis=-1, keepdims=True) + EPSILON)
    return values * inverse * norm_gain


def combine_partial(first, second):
    first_max, first_total, first_acc = first
    second_max, second_total, second_acc = second
    joint_max = jnp.maximum(first_max, second_max)
    first_scale = jnp.exp(first_max - joint_max)
    second_scale = jnp.exp(second_max - joint_max)
    joint_total = first_total * first_scale + second_total * second_scale
    joint_acc = first_acc * first_scale[..., None] + second_acc * second_scale[..., None]
    return (joint_max, joint_total, joint_acc)


def shards(
    tokens,
    lengths,
    assignment,
    retrieval,
    enc_gain,
    enc_qkv,
    position_bias,
    enc_output,
    final_gain,
    embedding,
    dec_tokens,
    dec_gain,
    cross_query,
    cross_keyval,
    cross_output,
):
    tok_rows = tokens.shape[0]
    model_width = tokens.shape[1]
    passages_here = lengths.shape[0]
    width_here = enc_qkv.shape[1]
    inner_here = enc_qkv.shape[2]
    heads_here = inner_here // HEAD_DIM
    query_rows = CLAIMS * POS
    positions = jnp.arange(SEQ)
    groups_count = lax.axis_size("mp")
    normed = rms_norm(tokens, enc_gain).astype(jnp.bfloat16)
    projected = jnp.einsum(
        "td,kdc->ktc",
        normed,
        lax.all_gather(enc_qkv, "psg", axis=1, tiled=True),
        preferred_element_type=jnp.float32,
    )
    shaped = projected.astype(jnp.bfloat16).reshape(3, passages_here, SEQ, heads_here, HEAD_DIM)
    bias_table = jnp.dot(
        position_bias, jnp.asarray(bucket_onehot(SEQ, BUCKETS, MAXDIST)), precision=HIGHEST
    )
    pair_bias = toeplitz(bias_table)
    scores = (
        jnp.einsum("pihd,pjhd->phij", shaped[0], shaped[1], preferred_element_type=jnp.float32)
        + pair_bias[None]
    )
    valid_keys = positions[None, :] < lengths[:, None]
    scores = jnp.where(valid_keys[:, None, None, :], scores, MASKED)
    weights = jnp.exp(scores - jnp.max(scores, axis=-1, keepdims=True))
    probabilities = (weights / jnp.sum(weights, axis=-1, keepdims=True)).astype(jnp.bfloat16)
    attended = jnp.einsum(
        "phij,pjhd->pihd", probabilities, shaped[2], preferred_element_type=jnp.float32
    )
    attended = attended.astype(jnp.bfloat16).reshape(tok_rows, inner_here)
    share_width = model_width // groups_count
    share_start = lax.axis_index("mp") * share_width
    partial_out = jnp.dot(
        attended,
        lax.all_gather(enc_output, "psg", axis=1, tiled=True),
        preferred_element_type=jnp.float32,
    ).astype(jnp.bfloat16)
    summed = lax.psum(partial_out, "mp").astype(jnp.float32)
    encoded_full = (tokens.astype(jnp.float32) + summed).astype(jnp.bfloat16)
    encoded = lax.dynamic_slice_in_dim(encoded_full, share_start, share_width, 1)
    memory = rms_norm(encoded_full, final_gain).astype(jnp.bfloat16)
    vocab_here = embedding.shape[0]
    token_ids = dec_tokens.reshape(-1) - lax.axis_index("mp") * vocab_here
    lookup = (token_ids[:, None] == jnp.arange(vocab_here)[None, :]).astype(jnp.bfloat16)
    found_rows = jnp.dot(lookup, embedding, preferred_element_type=jnp.float32).astype(jnp.bfloat16)
    embedded = lax.psum(found_rows, "mp").astype(jnp.float32)
    query_weight = cross_query.astype(jnp.float32)
    squares_dec = lax.psum(jnp.sum(embedded * embedded, axis=1), "psg")
    dquery = embedded * lax.rsqrt(squares_dec / D + EPSILON)[:, None] * dec_gain
    cquery = lax.psum(jnp.dot(dquery, query_weight, precision=HIGHEST), "psg")
    cquery = cquery.reshape(query_rows, heads_here, HEAD_DIM)
    row_claim = jnp.arange(query_rows) // POS
    usable = (row_claim[:, None, None] == assignment[None, :, None]) & (
        positions[None, None, :] < lengths[None, :, None]
    )
    usable = usable.reshape(query_rows, 1, tok_rows)
    key_bias = jnp.broadcast_to(retrieval[:, None], (passages_here, SEQ)).reshape(tok_rows)
    key_weight = cross_keyval[0].astype(jnp.float32).reshape(width_here, heads_here, HEAD_DIM)
    folded = jnp.einsum("rhj,dhj->rhd", cquery, key_weight, precision=HIGHEST)
    folded_all = lax.all_gather(folded.astype(jnp.bfloat16), "psg", axis=2, tiled=True).astype(
        folded.dtype
    )
    memory_wide = memory.astype(jnp.float32)
    cross_scores = jnp.einsum("td,rhd->rht", memory_wide, folded_all, precision=HIGHEST) + key_bias
    masked = jnp.where(usable, cross_scores, MASKED)
    local_max = jnp.max(masked, axis=-1)
    weights_c = jnp.where(usable, jnp.exp(masked - local_max[..., None]), 0.0)
    local_max, weights_c = (local_max, weights_c)
    local_total = jnp.sum(weights_c, axis=-1)
    pooled = jnp.einsum("rht,td->rhd", weights_c, memory_wide, precision=HIGHEST)
    joint_max, joint_total, joint_pool = merged(
        (local_max, local_total, pooled), "psg", combine_partial
    )
    own_pool = (
        lax.dynamic_slice_in_dim(joint_pool, lax.axis_index("psg") * width_here, width_here, 2)
        / joint_total[..., None]
    )
    value_weight = cross_keyval[1].astype(jnp.float32).reshape(width_here, heads_here, HEAD_DIM)
    value_terms = jnp.einsum("rhd,dhj->rhj", own_pool, value_weight, precision=HIGHEST)
    cross_attn = lax.psum(value_terms, "psg")
    out_part = jnp.dot(
        cross_attn.reshape(query_rows, inner_here),
        cross_output.astype(jnp.float32),
        precision=HIGHEST,
    )
    out_share = lax.psum_scatter(out_part, "mp", scatter_dimension=1, tiled=True)
    piece_width = out_share.shape[1]
    residual = lax.dynamic_slice_in_dim(
        embedded, lax.axis_index("mp") * piece_width, piece_width, 1
    )
    decoded = (residual + out_share).astype(jnp.bfloat16).reshape(CLAIMS, POS, piece_width)
    return (encoded, decoded)


def solution(mesh):
    in_specs = (
        P("psg", None),
        P("psg"),
        P("psg"),
        P("psg"),
        P(),
        P(None, "psg", "mp"),
        P("mp", None),
        P("mp", "psg"),
        P(),
        P("mp", "psg"),
        P(),
        P("psg"),
        P("psg", "mp"),
        P(None, "psg", "mp"),
        P("mp", "psg"),
    )
    out_specs = (P("psg", "mp"), P(None, None, ("psg", "mp")))
    return jax.shard_map(shards, mesh=mesh, in_specs=in_specs, out_specs=out_specs, check_vma=False)
```

profile of v0, /device:TPU:0, one launch (start us, length us, event | category | flops | bytes accessed | tf_op | source)
XLA Modules:
  0.0 641.4 jit_solution(5036497669544402802)
XLA Ops:
  12.6 7.9 %reshape.172 = f32[8,256,511]{2,1,0:T(8,128)} reshape(f32[8,130816]{1,0:T(8,128)} %slice.61) | data formatting | bytes 8372224 | tf_op jit(solution)/shard_map/reshape | solution.py:61
  24.9 5.1 fusion.7
  29.9 159.1 %all-gather.7.cloned.1.call-done = bf16[3,4096,512]{2,1,0:T(8,128)(2,1)} async-done(((bf16[3,512,512]{2,1,0:T(8,128)(2,1)}), bf16[3,4096,512]{2,1,0:T(8,128)(2,1)}) %all-gather.7.cloned.1.call-update) | async-done | bytes 12582928 | tf_op jit(solution)/shard_map/all_gather | solution.py:111
  189.0 18.3 %convert_bitcast_fusion = bf16[3,1024,512]{2,1,0:T(8,128)(2,1)S(1)} fusion(bf16[3,4096,512]{2,1,0:T(8,128)(2,1)} %all-gather.7.cloned.1.call-done, bf16[1024,4096]{1,0:T(8,128)(2,1)} %param.18, f32[4096]{0:T(1024)S(1)} %copy-done.10, f32[1024]{0:T(1024)S(1)} %add_rsqrt_fusion.1), kind=kOutput, calls=%fused_computation.37 | convolution fusion | flops 12903251968 | bytes 24137728 | tf_op jit(solution)/shard_map/td,kdc->ktc/dot_general | solution.py:108
  211.9 3.9 reshape.192
  215.8 3.9 reshape.190
  222.7 5.4 fusion.64
  228.0 4.5 fusion.35
  233.5 30.4 %all-gather.9.cloned.1.call-done = bf16[512,4096]{1,0:T(8,128)(2,1)} async-done(((bf16[512,512]{1,0:T(8,128)(2,1)}), bf16[512,4096]{1,0:T(8,128)(2,1)}) %all-gather.9.cloned.1.call-update) | async-done | bytes 4194320 | tf_op jit(solution)/shard_map/all_gather | solution.py:135
  263.9 8.9 %convolution_convert_fusion = bf16[1024,4096]{1,0:T(8,128)(2,1)} fusion(bf16[1024,512]{0,1:T(8,128)(2,1)S(1)} %bitcast.81, bf16[512,4096]{1,0:T(8,128)(2,1)} %all-gather.9.cloned.1.call-done), kind=kOutput, calls=%fused_computation.29 | convolution fusion | flops 4299161600 | bytes 13631488 | tf_op jit(solution)/shard_map/dot_general | solution.py:133
  273.7 5.1 convolution_convert_fusion.2
  278.8 6.7 %psum.36 = bf16[8,512]{1,0:T(8,128)(2,1)S(1)} all-reduce(bf16[8,512]{1,0:T(8,128)(2,1)S(1)} %convolution_convert_fusion.2), channel_id=1, replica_groups=mesh['psg'=8,'mp'=4] {'mp'}, use_global_device_ids=true, to_apply=%region_4.5 | all-reduce | flops 4096 | bytes 16384 | tf_op jit(solution)/shard_map/psum | solution.py:146
  285.7 19.2 %psum.37 = f32[8]{0:T(128)S(1)} all-reduce(f32[8]{0:T(128)S(1)} %multiply_reduce_fusion), channel_id=1, replica_groups=mesh['psg'=8,'mp'=4] {'psg'}, use_global_device_ids=true, to_apply=%region_6.7 | all-reduce | flops 8 | bytes 64 | tf_op jit(solution)/shard_map/psum | solution.py:148
  305.8 33.1 %psum.38 = f32[8,8,64]{2,0,1:T(8,128)S(1)} all-reduce(f32[8,8,64]{2,0,1:T(8,128)S(1)} %copy.49), channel_id=1, replica_groups=mesh['psg'=8,'mp'=4] {'psg'}, use_global_device_ids=true, to_apply=%region_7.8 | all-reduce | flops 4096 | bytes 32768 | tf_op jit(solution)/shard_map/psum | solution.py:150
  339.4 31.5 %all_gather.29 = bf16[8,8,4096]{2,0,1:T(8,128)(2,1)S(1)} all-gather(bf16[8,8,512]{2,0,1:T(8,128)(2,1)S(1)} %fusion.44), channel_id=1, replica_groups=mesh['psg'=8,'mp'=4] {'psg'}, dimensions={2}, use_global_device_ids=true | all-gather | bytes 589824 | tf_op jit(solution)/shard_map/all_gather | solution.py:160
  370.9 53.5 %all-reduce.3.cloned.1.call-done = bf16[1024,4096]{1,0:T(8,128)(2,1)} async-done(((bf16[1024,4096]{1,0:T(8,128)(2,1)}), bf16[1024,4096]{1,0:T(8,128)(2,1)}) %all-reduce.3.cloned.1.call-update) | async-done | bytes 8388624 | tf_op jit(solution)/shard_map/psum | solution.py:138
  424.4 7.8 %fusion.4 = (f32[1024]{0:T(1024)S(1)}, bf16[1024,4096]{1,0:T(8,128)(2,1)S(1)}) fusion(bf16[1024,4096]{1,0:T(8,128)(2,1)} %all-reduce.3.cloned.1.call-done, bf16[1024,4096]{1,0:T(8,128)(2,1)} %param.18), kind=kLoop, calls=%fused_computation.14 | loop fusion | flops 29359104 | bytes 25169920 | tf_op jit(solution)/shard_map/reduce_sum | solution.py:66
  435.4 6.4 %fusion.18 = f32[8,8,4096]{2,1,0:T(8,128)} fusion(bf16[1024,4096]{1,0:T(8,128)(2,1)S(1)} %get-tuple-element.200, f32[4096]{0:T(1024)S(1)} %copy-done.11, f32[1024]{0:T(1024)S(1)} %add_rsqrt_fusion, f32[8,8,1024]{2,1,0:T(8,128)S(1)} %get-tuple-element.209, f32[8,8]{1,0:T(8,128)S(1)} %get-tuple-element.208, pred[8,1024]{1,0:T(8,128)(4,1)S(1)} %broadcast_and_fusion), kind=kOutput, calls=%fused_computation.31 | convolution fusion | flops 3238133760 | bytes 9728256 | tf_op jit(solution)/shard_map/rht,td->rhd/dot_general | solution.py:170
  442.3 31.6 %all-gather.1 = f32[64,8]{1,0:T(8,128)S(1)} all-gather(f32[8,8]{1,0:T(8,128)S(1)} %fusion.46), channel_id=3, replica_groups=mesh['psg'=8,'mp'=4] {'psg'}, dimensions={0}, use_global_device_ids=true | all-gather | bytes 2304 | tf_op jit(solution)/shard_map/all_gather | solution.py:21
  474.0 31.6 %all-gather = f32[64,8]{1,0:T(8,128)S(1)} all-gather(f32[8,8]{1,0:T(8,128)S(1)} %get-tuple-element.208), channel_id=2, replica_groups=mesh['psg'=8,'mp'=4] {'psg'}, dimensions={0}, use_global_device_ids=true | all-gather | bytes 2304 | tf_op jit(solution)/shard_map/all_gather | solution.py:21
  505.6 61.5 %all-gather.11.cloned.1.call-done = f32[64,8,4096]{2,1,0:T(8,128)} async-done(((f32[8,8,4096]{2,1,0:T(8,128)}), f32[64,8,4096]{2,1,0:T(8,128)}) %all-gather.11.cloned.1.call-update) | async-done | bytes 8388624 | tf_op jit(solution)/shard_map/all_gather | solution.py:21
  568.4 12.4 %while.19 = (s32[]{:T(128)}, f32[8,8]{1,0:T(8,128)S(1)}, f32[8,8]{1,0:T(8,128)S(1)}, f32[8,8,4096]{2,1,0:T(8,128)S(1)}, f32[8,8,8]{2,1,0:T(8,128)S(1)}, /*index=...) while((s32[]{:T(128)}, f32[8,8]{1,0:T(8,128)S(1)}, ...), condition=%wide.region_12.13_spmd, body=%wide.region_11.12_spmd.sunk | while | flops 786821 | bytes 3148439 | solution.py:27
  581.5 34.2 %psum.39 = f32[8,512]{1,0:T(8,128)S(1)} all-reduce(f32[8,512]{1,0:T(8,128)S(1)} %reshape.177), channel_id=1, replica_groups=mesh['psg'=8,'mp'=4] {'psg'}, use_global_device_ids=true, to_apply=%region_13.14 | all-reduce | flops 4096 | bytes 32768 | tf_op jit(solution)/shard_map/psum | solution.py:180
  619.8 13.8 %reduce-scatter.2.cloned.1.call-done = f32[8,128]{1,0:T(8,128)} async-done(((f32[8,512]{1,0:T(8,128)}), f32[8,128]{1,0:T(8,128)}) %reduce-scatter.2.cloned.1.call-update) | async-done | bytes 4112 | tf_op jit(solution)/shard_map/reduce_scatter | solution.py:186
  (101 shorter events, 43.8 us)
Async XLA Ops:
  7.2 297.7 %copy-start = (bf16[512,512]{1,0:T(8,128)(2,1)S(1)}, bf16[512,512]{1,0:T(8,128)(2,1)}, u32[]{:S(2)}) copy-start(bf16[512,512]{1,0:T(8,128)(2,1)} %param.30) | copy-start | bytes 1572868
  7.2 181.8 %all-gather.7.cloned.1.call-start = ((), (), s32[]{:S(2)}) async-start(), calls=%async_computation.1 | async-start | bytes 14155776 | tf_op jit(solution)/shard_map/all_gather | solution.py:111
  7.9 256.0 %all-gather.9.cloned.1.call-start = ((), (), s32[]{:S(2)}) async-start(), calls=%async_computation.2 | async-start | bytes 4718592 | tf_op jit(solution)/shard_map/all_gather | solution.py:135
  8.7 415.7 %all-reduce.3.cloned.1.call-start = ((), (), s32[]{:S(2)}) async-start(), calls=%async_computation.3 | async-start | bytes 16777216 | tf_op jit(solution)/shard_map/psum | solution.py:138
  12.6 12.1 %copy-start.9 = (s32[4]{0:T(128)S(1)}, s32[4]{0:T(128)}, u32[]{:S(2)}) copy-start(s32[4]{0:T(128)} %param.19) | copy-start | bytes 52
  20.5 168.5 %copy-start.10 = (f32[4096]{0:T(1024)S(1)}, f32[4096]{0:T(1024)}, u32[]{:S(2)}) copy-start(f32[4096]{0:T(1024)} %param.22) | copy-start | bytes 49156
  219.6 3.0 copy-start.3
  222.7 5.4 copy-start.2
  272.8 0.7 copy-start.7
  272.9 32.0 %copy-start.6 = (f32[512]{0:T(512)S(1)}, f32[512]{0:T(512)}, u32[]{:S(2)}) copy-start(f32[512]{0:T(512)} %param.29) | copy-start | bytes 6148
  272.9 32.4 %copy-start.4 = (bf16[2,512,512]{2,1,0:T(8,128)(2,1)S(1)}, bf16[2,512,512]{2,1,0:T(8,128)(2,1)}, u32[]{:S(2)}) copy-start(bf16[2,512,512]{2,1,0:T(8,128)(2,1)} %param.31) | copy-start | bytes 3145732
  272.9 294.2 %all-gather.11.cloned.1.call-start = ((), (), s32[]{:S(2)}) async-start(), calls=%async_computation.5 | async-start | bytes 9437184 | tf_op jit(solution)/shard_map/all_gather | solution.py:21
  273.7 31.9 %copy-start.8 = (f32[4]{0:T(128)S(1)}, f32[4]{0:T(128)}, u32[]{:S(2)}) copy-start(f32[4]{0:T(128)} %param.21) | copy-start | bytes 52
  273.7 65.2 %copy-start.12 = (s32[4]{0:T(128)S(1)}, s32[4]{0:T(128)}, u32[]{:S(2)}) copy-start(s32[4]{0:T(128)} %param.20) | copy-start | bytes 52
  370.9 61.3 %copy-start.11 = (f32[4096]{0:T(1024)S(1)}, f32[4096]{0:T(1024)}, u32[]{:S(2)}) copy-start(f32[4096]{0:T(1024)} %param.26) | copy-start | bytes 49156
  432.2 3.2 copy-start.1
  441.9 191.8 %reduce-scatter.2.cloned.1.call-start = ((), (), s32[]{:S(2)}) async-start(), calls=%async_computation.4 | async-start | bytes 20480 | tf_op jit(solution)/shard_map/reduce_scatter | solution.py:186
  568.4 47.4 %copy-start.5 = (bf16[512,512]{1,0:T(8,128)(2,1)S(1)}, bf16[512,512]{1,0:T(8,128)(2,1)}, u32[]{:S(2)}) copy-start(bf16[512,512]{1,0:T(8,128)(2,1)} %param.32) | copy-start | bytes 1572868
Sparse Core Ops, SparseCore 0:
  10.2 178.8 all-gather.6
  191.1 72.8 all-gather.8
  273.0 151.3 all-reduce.2
  442.0 125.0 all-gather.10
  616.8 16.7 reduce-scatter.1
where the time goes:
time: 642 us; the launch traced here: 641 us
  waiting for transfers between devices  320 us (50%)
  blocking collectives  188 us (29%)
  matrix products  52.2 us (8%)
  local copies, waits for them, and re-layouts  34.7 us (5%)
  other arithmetic  32.4 us (5%)
  between operations  14.1 us (2%)
    all_gather x1, waiting for transfers between devices, shards(): lax.all_gather(enc_qkv, 'psg', axis=1, tiled=True)  159 us
    all_gather x2, blocking collectives, merged(): everything = jax.tree.map(lambda part: lax.all_gather(part, axis), value)  63.2 us
    all_gather x1, waiting for transfers between devices, merged(): everything = jax.tree.map(lambda part: lax.all_gather(part, axis), value)  61.5 us
    psum x1, waiting for transfers between devices, shards(): summed = lax.psum(partial_out, 'mp').astype(jnp.float32)  53.5 us
    psum x1, blocking collectives, shards(): cross_attn = lax.psum(value_terms, 'psg')  34.2 us
    psum x1, blocking collectives, shards(): cquery = lax.psum(jnp.dot(dquery, query_weight, precision=HIGHEST), 'psg')  33.1 us
    all_gather x1, blocking collectives, shards(): lax.all_gather(folded.astype(jnp.bfloat16), 'psg', axis=2, tiled=True)  31.5 us
    all_gather x1, waiting for transfers between devices, shards(): lax.all_gather(enc_output, 'psg', axis=1, tiled=True)  30.4 us
  transfers between devices with their start and end apart: 5, of which 5 were waited for; matrix products, arithmetic and copies ran while one was open for 12% of the time, Pallas kernels for 0%

commit v1 on v0

--- a/solution.py
+++ b/solution.py
@@ -15,6 +15,18 @@
 EPSILON = 1e-06
 MASKED = -1e30
 HIGHEST = lax.Precision.HIGHEST
+
+
+def doubled_up(array, axis, dim):
+    ways, here = (lax.axis_size(axis), lax.axis_index(axis))
+    grown, reach = (array, 1)
+    while reach < ways:
+        theirs = lax.ppermute(grown, axis, [(d, d ^ reach) for d in range(ways)])
+        mine_first = jnp.concatenate([grown, theirs], axis=dim)
+        theirs_first = jnp.concatenate([theirs, grown], axis=dim)
+        grown = jnp.where(here & reach == 0, mine_first, theirs_first)
+        reach = 2 * reach
+    return grown
 
 
 def merged(value, axis, combine):
@@ -106,10 +118,7 @@
     groups_count = lax.axis_size("mp")
     normed = rms_norm(tokens, enc_gain).astype(jnp.bfloat16)
     projected = jnp.einsum(
-        "td,kdc->ktc",
-        normed,
-        lax.all_gather(enc_qkv, "psg", axis=1, tiled=True),
-        preferred_element_type=jnp.float32,
+        "td,kdc->ktc", normed, doubled_up(enc_qkv, "psg", 1), preferred_element_type=jnp.float32
     )
     shaped = projected.astype(jnp.bfloat16).reshape(3, passages_here, SEQ, heads_here, HEAD_DIM)
     bias_table = jnp.dot(

time: 642 us -> 873 us (1.36)
  waiting for transfers between devices: 320 us -> 531 us
  other arithmetic: 32.4 us -> 45.6 us
    ppermute x0 -> x3, waiting for transfers between devices: none -> 402 us  [doubled_up(): theirs = lax.ppermute(grown, axis, [(d, d ^ reach) for d in range(ways)])]
    all_gather x1 -> x0, waiting for transfers between devices: 159 us -> none  [shards(): lax.all_gather(enc_qkv, 'psg', axis=1, tiled=True)]
    all_gather x1, waiting for transfers between devices: 30.4 us -> 0.02 us  [shards(): lax.all_gather(enc_output, 'psg', axis=1, tiled=True)]
    select_n x0 -> x2, other arithmetic: none -> 13.2 us  [doubled_up(): grown = jnp.where(here & reach == 0, mine_first, theirs_first)]
  transfers between devices with their start and end apart: 5 -> 7, of which waited for: 5 -> 6; matrix products, arithmetic and copies ran while one was open for 12% -> 8% of each run, Pallas kernels for 0% -> 0%
where the time goes in v1:
time: 873 us
  waiting for transfers between devices  531 us (61%)
  blocking collectives  191 us (22%)
  matrix products  51.8 us (6%)
  other arithmetic  45.6 us (5%)
  local copies, waits for them, and re-layouts  31.1 us (4%)
  between operations  14.1 us (2%)
    ppermute x3, waiting for transfers between devices, doubled_up(): theirs = lax.ppermute(grown, axis, [(d, d ^ reach) for d in range(ways)])  402 us
    all_gather x2, blocking collectives, merged(): everything = jax.tree.map(lambda part: lax.all_gather(part, axis), value)  63.2 us
    all_gather x1, waiting for transfers between devices, merged(): everything = jax.tree.map(lambda part: lax.all_gather(part, axis), value)  61.5 us
    psum x1, waiting for transfers between devices, shards(): summed = lax.psum(partial_out, 'mp').astype(jnp.float32)  53.4 us
    psum x1, blocking collectives, shards(): cross_attn = lax.psum(value_terms, 'psg')  34.2 us
    psum x1, blocking collectives, shards(): cquery = lax.psum(jnp.dot(dquery, query_weight, precision=HIGHEST), 'psg')  33.2 us
    all_gather x1, blocking collectives, shards(): lax.all_gather(folded.astype(jnp.bfloat16), 'psg', axis=2, tiled=True)  31.5 us
    psum x1, blocking collectives, shards(): squares_dec = lax.psum(jnp.sum(embedded * embedded, axis=1), 'psg')  22.3 us
  transfers between devices with their start and end apart: 7, of which 6 were waited for; matrix products, arithmetic and copies ran while one was open for 8% of the time, Pallas kernels for 0%

profile of v1, /device:TPU:0, one launch (start us, length us, event | category | flops | bytes accessed | tf_op | source)
XLA Modules:
  0.0 872.5 jit_solution(9287941861875749332)
XLA Ops:
  10.3 34.6 %collective-permute-done = bf16[3,512,512]{2,1,0:T(8,128)(2,1)S(1)} collective-permute-done((bf16[3,512,512]{2,1,0:T(8,128)(2,1)}, bf16[3,512,512]{2,1,0:T(8,128)(2,1)S(1)}, u32[]{:S(2)}, u32[]{:S(2)}) %collective-permute-start) | collective-permute-done | bytes 1572896 | tf_op jit(solution)/shard_map/ppermute | solution.py:24
  50.3 67.8 %collective-permute-done.1 = bf16[3,1024,512]{2,1,0:T(8,128)(2,1)} collective-permute-done((bf16[3,1024,512]{2,1,0:T(8,128)(2,1)}, bf16[3,1024,512]{2,1,0:T(8,128)(2,1)}, u32[]{:S(2)}, u32[]{:S(2)}) %collective-permute-start.1) | collective-permute-done | bytes 3145760 | tf_op jit(solution)/shard_map/ppermute | solution.py:24
  118.0 9.6 %maximum_select_fusion.2 = bf16[3,2048,512]{2,1,0:T(8,128)(2,1)} fusion(bf16[3,1024,512]{2,1,0:T(8,128)(2,1)} %collective-permute-done.1, bf16[3,1024,512]{2,1,0:T(8,128)(2,1)} %maximum_select_fusion.3, pred[]{:T(512)S(6)} %eq.41), kind=kLoop, calls=%fused_computation.38 | loop fusion | flops 28311552 | bytes 12582913 | tf_op jit(solution)/shard_map/jit(_where)/select_n | solution.py:27
  133.5 7.9 reshape.172
  145.2 5.1 fusion.7
  150.3 299.9 %collective-permute-done.2 = bf16[3,2048,512]{2,1,0:T(8,128)(2,1)} collective-permute-done((bf16[3,2048,512]{2,1,0:T(8,128)(2,1)}, bf16[3,2048,512]{2,1,0:T(8,128)(2,1)}, u32[]{:S(2)}, u32[]{:S(2)}) %collective-permute-start.2) | collective-permute-done | bytes 6291488 | tf_op jit(solution)/shard_map/ppermute | solution.py:24
  450.2 21.1 %convert_bitcast_fusion = bf16[3,1024,512]{1,2,0:T(8,128)(2,1)} fusion(bf16[1024,4096]{1,0:T(8,128)(2,1)} %param.18, f32[4096]{0:T(1024)S(1)} %copy-done.12, f32[1024]{0:T(1024)S(1)} %add_rsqrt_fusion.1, bf16[3,2048,512]{2,1,0:T(8,128)(2,1)} %collective-permute-done.2, bf16[3,2048,512]{2,1,0:T(8,128)(2,1)} %maximum_select_fusion.2, pred[]{:T(512)S(6)} %eq.40), kind=kOutput, calls=%fused_computation.46 | convolution fusion | flops 12959875072 | bytes 24137728 | tf_op jit(solution)/shard_map/td,kdc->ktc/dot_general | solution.py:120
  481.8 5.3 fusion.67
  487.1 4.2 fusion.35
  492.4 9.0 %convolution_convert_fusion = bf16[1024,4096]{1,0:T(8,128)(2,1)} fusion(bf16[1024,512]{0,1:T(8,128)(2,1)S(1)} %bitcast.86, bf16[512,4096]{1,0:T(8,128)(2,1)} %all-gather.6.cloned.1.call-done), kind=kOutput, calls=%fused_computation.36 | convolution fusion | flops 4299161600 | bytes 13631488 | tf_op jit(solution)/shard_map/dot_general | solution.py:142
  502.2 4.6 convolution_convert_fusion.2
  506.8 6.7 psum.36
  513.6 22.3 %psum.37 = f32[8]{0:T(128)S(1)} all-reduce(f32[8]{0:T(128)S(1)} %multiply_reduce_fusion), channel_id=1, replica_groups=mesh['psg'=8,'mp'=4] {'psg'}, use_global_device_ids=true, to_apply=%region_6.7 | all-reduce | flops 8 | bytes 64 | tf_op jit(solution)/shard_map/psum | solution.py:157
  536.9 33.2 %psum.38 = f32[8,8,64]{2,0,1:T(8,128)S(1)} all-reduce(f32[8,8,64]{2,0,1:T(8,128)S(1)} %copy.46), channel_id=1, replica_groups=mesh['psg'=8,'mp'=4] {'psg'}, use_global_device_ids=true, to_apply=%region_7.8 | all-reduce | flops 4096 | bytes 32768 | tf_op jit(solution)/shard_map/psum | solution.py:159
  570.5 31.5 %all_gather.25 = bf16[8,8,4096]{2,0,1:T(8,128)(2,1)S(1)} all-gather(bf16[8,8,512]{2,0,1:T(8,128)(2,1)S(1)} %fusion.42), channel_id=1, replica_groups=mesh['psg'=8,'mp'=4] {'psg'}, dimensions={2}, use_global_device_ids=true | all-gather | bytes 589824 | tf_op jit(solution)/shard_map/all_gather | solution.py:169
  602.1 53.4 %all-reduce.3.cloned.1.call-done = bf16[1024,4096]{1,0:T(8,128)(2,1)} async-done(((bf16[1024,4096]{1,0:T(8,128)(2,1)}), bf16[1024,4096]{1,0:T(8,128)(2,1)}) %all-reduce.3.cloned.1.call-update) | async-done | bytes 8388624 | tf_op jit(solution)/shard_map/psum | solution.py:147
  655.5 7.8 fusion.4
  666.5 6.4 fusion.24
  673.5 31.6 %all-gather.1 = f32[64,8]{1,0:T(8,128)S(1)} all-gather(f32[8,8]{1,0:T(8,128)S(1)} %fusion.48), channel_id=3, replica_groups=mesh['psg'=8,'mp'=4] {'psg'}, dimensions={0}, use_global_device_ids=true | all-gather | bytes 2304 | tf_op jit(solution)/shard_map/all_gather | solution.py:33
  705.1 31.6 %all-gather = f32[64,8]{1,0:T(8,128)S(1)} all-gather(f32[8,8]{1,0:T(8,128)S(1)} %get-tuple-element.208), channel_id=2, replica_groups=mesh['psg'=8,'mp'=4] {'psg'}, dimensions={0}, use_global_device_ids=true | all-gather | bytes 2304 | tf_op jit(solution)/shard_map/all_gather | solution.py:33
  736.7 61.5 %all-gather.8.cloned.1.call-done = f32[64,8,4096]{2,1,0:T(8,128)} async-done(((f32[8,8,4096]{2,1,0:T(8,128)}), f32[64,8,4096]{2,1,0:T(8,128)}) %all-gather.8.cloned.1.call-update) | async-done | bytes 8388624 | tf_op jit(solution)/shard_map/all_gather | solution.py:33
  799.5 12.4 %while.19 = (s32[]{:T(128)}, f32[8,8]{1,0:T(8,128)S(1)}, f32[8,8]{1,0:T(8,128)S(1)}, f32[8,8,4096]{2,1,0:T(8,128)S(1)}, f32[8,8,8]{2,1,0:T(8,128)S(1)}, /*index=...) while((s32[]{:T(128)}, f32[8,8]{1,0:T(8,128)S(1)}, ...), condition=%wide.region_12.13_spmd, body=%wide.region_11.12_spmd.sunk | while | flops 786821 | bytes 3148439 | solution.py:39
  812.6 34.2 %psum.39 = f32[8,512]{1,0:T(8,128)S(1)} all-reduce(f32[8,512]{1,0:T(8,128)S(1)} %reshape.177), channel_id=1, replica_groups=mesh['psg'=8,'mp'=4] {'psg'}, use_global_device_ids=true, to_apply=%region_13.14 | all-reduce | flops 4096 | bytes 32768 | tf_op jit(solution)/shard_map/psum | solution.py:189
  850.9 13.8 %reduce-scatter.2.cloned.1.call-done = f32[8,128]{1,0:T(8,128)} async-done(((f32[8,512]{1,0:T(8,128)}), f32[8,128]{1,0:T(8,128)}) %reduce-scatter.2.cloned.1.call-update) | async-done | bytes 4112 | tf_op jit(solution)/shard_map/reduce_scatter | solution.py:195
  (110 shorter events, 55.1 us)
Async XLA Ops:
  7.2 528.8 %copy-start = (bf16[512,512]{1,0:T(8,128)(2,1)S(1)}, bf16[512,512]{1,0:T(8,128)(2,1)}, u32[]{:S(2)}) copy-start(bf16[512,512]{1,0:T(8,128)(2,1)} %param.30) | copy-start | bytes 1572868
  7.2 485.2 %all-gather.6.cloned.1.call-start = ((), (), s32[]{:S(2)}) async-start(), calls=%async_computation.1 | async-start | bytes 4718592 | tf_op jit(solution)/shard_map/all_gather | solution.py:144
  7.2 37.6 %collective-permute-start = (bf16[3,512,512]{2,1,0:T(8,128)(2,1)}, bf16[3,512,512]{2,1,0:T(8,128)(2,1)S(1)}, u32[]{:S(2)}, u32[]{:S(2)}) collective-permute-start(bf16[3,512,512]{2,1,0:T(8,128)(2,1)} %param.23), channel_id=1, source_target_pairs={{0,4},{4,0},{8,12},{12,8},{16,20},{20,16},{24,28},{28,24},{1,5},{5... | collective-permute-start | bytes 4718600 | tf_op jit(solution)/shard_map/ppermute | solution.py:24
  10.3 120.0 %copy-start.6 = (f32[32,511]{1,0:T(8,128)S(1)}, f32[32,511]{1,0:T(8,128)}, u32[]{:S(2)}) copy-start(f32[32,511]{1,0:T(8,128)} %constant.93.clone) | copy-start | bytes 196228
  10.3 120.0 %copy-start.7 = (f32[8,32]{1,0:T(8,128)S(1)}, f32[8,32]{1,0:T(8,128)}, u32[]{:S(2)}) copy-start(f32[8,32]{1,0:T(8,128)} %param.24) | copy-start | bytes 3076
  10.3 120.3 %copy-start.11 = (s32[4]{0:T(128)S(1)}, s32[4]{0:T(128)}, u32[]{:S(2)}) copy-start(s32[4]{0:T(128)} %param.19) | copy-start | bytes 52
  48.4 69.6 %collective-permute-start.1 = (bf16[3,1024,512]{2,1,0:T(8,128)(2,1)}, bf16[3,1024,512]{2,1,0:T(8,128)(2,1)}, u32[]{:S(2)}, u32[]{:S(2)}) collective-permute-start(bf16[3,1024,512]{2,1,0:T(8,128)(2,1)} %maximum_select_fusion.3), channel_id=1, source_target_pairs={{0,8},{4,12},{8,0},{12,4},{16,24},{20,28},{24,16},{28,20},{1,9},{5... | collective-permute-start | bytes 9437192 | tf_op jit(solution)/shard_map/ppermute | solution.py:24
  127.6 322.5 %collective-permute-start.2 = (bf16[3,2048,512]{2,1,0:T(8,128)(2,1)}, bf16[3,2048,512]{2,1,0:T(8,128)(2,1)}, u32[]{:S(2)}, u32[]{:S(2)}) collective-permute-start(bf16[3,2048,512]{2,1,0:T(8,128)(2,1)} %maximum_select_fusion.2), channel_id=1, source_target_pairs={{0,16},{4,20},{8,24},{12,28},{16,0},{20,4},{24,8},{28,12},{1,17},{... | collective-permute-start | bytes 18874376 | tf_op jit(solution)/shard_map/ppermute | solution.py:24
  130.2 525.2 %all-reduce.3.cloned.1.call-start = ((), (), s32[]{:S(2)}) async-start(), calls=%async_computation.2 | async-start | bytes 16777216 | tf_op jit(solution)/shard_map/psum | solution.py:147
  141.3 308.9 %copy-start.12 = (f32[4096]{0:T(1024)S(1)}, f32[4096]{0:T(1024)}, u32[]{:S(2)}) copy-start(f32[4096]{0:T(1024)} %param.22) | copy-start | bytes 49156
  480.2 1.6 copy-start.2
  481.8 5.3 copy-start.4
  501.4 0.7 copy-start.9
  501.4 34.5 %copy-start.8 = (f32[512]{0:T(512)S(1)}, f32[512]{0:T(512)}, u32[]{:S(2)}) copy-start(f32[512]{0:T(512)} %param.29) | copy-start | bytes 6148
  501.4 35.0 %copy-start.3 = (bf16[2,512,512]{2,1,0:T(8,128)(2,1)S(1)}, bf16[2,512,512]{2,1,0:T(8,128)(2,1)}, u32[]{:S(2)}) copy-start(bf16[2,512,512]{2,1,0:T(8,128)(2,1)} %param.31) | copy-start | bytes 3145732
  501.4 296.8 %all-gather.8.cloned.1.call-start = ((), (), s32[]{:S(2)}) async-start(), calls=%async_computation.4 | async-start | bytes 9437184 | tf_op jit(solution)/shard_map/all_gather | solution.py:33
  502.2 34.5 %copy-start.10 = (f32[4]{0:T(128)S(1)}, f32[4]{0:T(128)}, u32[]{:S(2)}) copy-start(f32[4]{0:T(128)} %param.21) | copy-start | bytes 52
  502.2 67.8 %copy-start.14 = (s32[4]{0:T(128)S(1)}, s32[4]{0:T(128)}, u32[]{:S(2)}) copy-start(s32[4]{0:T(128)} %param.20) | copy-start | bytes 52
  602.0 61.3 %copy-start.13 = (f32[4096]{0:T(1024)S(1)}, f32[4096]{0:T(1024)}, u32[]{:S(2)}) copy-start(f32[4096]{0:T(1024)} %param.26) | copy-start | bytes 49156
  663.3 3.2 copy-start.1
  673.0 191.8 %reduce-scatter.2.cloned.1.call-start = ((), (), s32[]{:S(2)}) async-start(), calls=%async_computation.3 | async-start | bytes 20480 | tf_op jit(solution)/shard_map/reduce_scatter | solution.py:195
  799.5 47.4 %copy-start.5 = (bf16[512,512]{1,0:T(8,128)(2,1)S(1)}, bf16[512,512]{1,0:T(8,128)(2,1)}, u32[]{:S(2)}) copy-start(bf16[512,512]{1,0:T(8,128)(2,1)} %param.32) | copy-start | bytes 1572868
Sparse Core Ops, SparseCore 0:
  130.3 219.9 all-gather.5
  501.5 153.9 all-reduce.2
  673.1 125.0 all-gather.7
  847.9 16.7 reduce-scatter.1
